TPU v7x, 512 devices: a whole 4x4x16 slice. The times are simulated.
512 devices in a mesh: user: 512 (over z, x, y, core).
Axes of the slice: x: 4, y: 4, z: 16, core: 2. Of those that a mesh axis runs over, the one named last changes fastest.
Arguments:
- ratings: bfloat16 [512, 3, 6, 128, 128], P('user'), may hold values from -6 to 6
- tile_index: int32 [512, 3, 6], P('user'), may hold values from 0 to 8, as said below
- tile_count: int32 [512, 3], P('user'), may hold values from 1 to 6, as said below
- side_features: bfloat16 [196608, 1024], P('user'), may hold values from -6 to 6
- user_factors: float32 [196608, 256], P('user'), may hold values from -3 to 3
- item_factors: float32 [196608, 256], P('user'), may hold values from -3 to 3
- prior_weights: float32 [1024, 256], replicated, may hold values from -0.1875 to 0.1875
- user_noise: bfloat16 [3, 196608, 256], P(None, 'user'), may hold values from -6 to 6
- item_noise: bfloat16 [3, 196608, 256], P(None, 'user'), may hold values from -6 to 6
Outputs:
- users_out: float32 [196608, 256], P('user')
- items_held: float32 [196608, 256], P('user')
- weights_out: float32 [1024, 256], P('user')
Inputs may be any that keep to these rules, and one draw needn't show every extreme that they name: `tile_index`: code r * 3 + c of a tile; the codes of one device and stratum are distinct. `tile_count`: live slots are the first ones; in every stratum some device has 6.
All inputs are finite; a program needn't handle non-finite values.
Results may differ from a plain program's by a relative error of at most 0.0013.
The roundings to bfloat16 on the way count: a program that leaves them out, or rounds other values in their place, can miss the bound.
Values sent between devices are 32-bit elements; how exact they have to be, the bound alone decides.
A program may use at most 64 MiB of HBM per device.

v0:
```python
import math

import jax
import jax.numpy as jnp
from jax import lax
from jax.sharding import Mesh
from jax.sharding import PartitionSpec as P

USER = ("user_0", "user_1", "user_2", "user_3")


step_size = 0.01
prior_prec = 8.0
item_prec = 1.0
weight_decay = 1.0
rate_scale = 0.04


def from_everyone(array, axis):
    devices = lax.axis_size(axis)
    return lax.all_to_all(
        jnp.broadcast_to(array[None], (devices, *array.shape)), axis, 0, 0, tiled=True
    )


def over_copies(array, axis):
    everything = from_everyone(array, axis)
    return jnp.sum(everything, axis=0)


def one_axis_at_a_time(array, axes):
    far, near = axes
    return over_copies(over_copies(array, near), far)


def packed_total(arrays, axis):
    ends = [0]
    for a in arrays:
        ends.append(ends[-1] + a.size)
    subtotal = one_axis_at_a_time(jnp.concatenate([a.ravel() for a in arrays]), axis)
    return tuple((subtotal[b:e].reshape(a.shape) for a, b, e in zip(arrays, ends, ends[1:])))


def padded_to(lines, devices):
    spare = -lines.shape[0] % devices
    if not spare:
        return lines
    return jnp.concatenate([lines, jnp.zeros((spare, *lines.shape[1:]), lines.dtype)])


def joined_along(tiles, dim):
    shape = list(tiles.shape[1:])
    shape[dim] *= tiles.shape[0]
    return jnp.moveaxis(tiles, 0, dim).reshape(shape)


def gathered_by_axis(array, axes, dim):
    far, near = axes
    tiles = from_everyone(from_everyone(array, far), near)
    return joined_along(tiles.swapaxes(0, 1).reshape(-1, *array.shape), dim)


def in_blocks(array, dim, devices):
    before, after = (array.shape[:dim], array.shape[dim + 1 :])
    return jnp.moveaxis(array.reshape(*before, devices, -1, *after), dim, 0)


def sum_at_owner(array, axis, dim):
    devices = lax.axis_size(axis)
    tiles = lax.all_to_all(in_blocks(array, dim, devices), axis, 0, 0, tiled=True)
    return jnp.sum(tiles, axis=0)


def sum_by_axis(array, axes, dim):
    far, near = axes
    tiles = in_blocks(array, dim, lax.axis_size(far))
    nearer = sum_at_owner(tiles, near, dim + 1)
    arrived = lax.all_to_all(nearer, far, split_axis=0, concat_axis=0, tiled=True)
    return arrived.sum(axis=0)


def total_of(array, axes):
    lines = array.reshape(-1, array.shape[-1])
    padded = padded_to(lines, lax.axis_size(axes[0]) * lax.axis_size(axes[1]))
    whole = gathered_by_axis(sum_by_axis(padded, axes, 0), axes, 0)
    return lax.slice_in_dim(whole, 0, len(lines)).reshape(array.shape)


def shifted(array, axis, by):
    devices = lax.axis_size(axis)
    return lax.ppermute(array, axis, [(i, (i + by) % devices) for i in range(devices)])


def tile_pass(tiles, codes, count, user_b, item_b):
    tile = tiles.shape[-1]
    grid = user_b.shape[0] // tile
    slots = tiles.shape[0]

    def one(step, carry):
        sse, grad_u, grad_v = carry
        code = codes[step]
        row_start = code // grid * tile
        col_start = code % grid * tile
        user_tile = lax.dynamic_slice_in_dim(user_b, row_start, tile, 0)
        item_tile = lax.dynamic_slice_in_dim(item_b, col_start, tile, 0)
        pred = lax.dot_general(
            user_tile, item_tile, (((1,), (1,)), ((), ())), preferred_element_type=jnp.float32
        )
        err = lax.dynamic_index_in_dim(tiles, step, 0, keepdims=False).astype(jnp.float32) - pred
        err = err * (step < count).astype(jnp.float32)
        sse = sse + jnp.sum(err * err)
        err_b = err.astype(jnp.bfloat16)
        upd_u = jnp.dot(err_b, item_tile, preferred_element_type=jnp.float32)
        upd_v = lax.dot_general(
            err_b, user_tile, (((0,), (0,)), ((), ())), preferred_element_type=jnp.float32
        )
        grad_u = lax.dynamic_update_slice_in_dim(
            grad_u, lax.dynamic_slice_in_dim(grad_u, row_start, tile, 0) + upd_u, row_start, 0
        )
        grad_v = lax.dynamic_update_slice_in_dim(
            grad_v, lax.dynamic_slice_in_dim(grad_v, col_start, tile, 0) + upd_v, col_start, 0
        )
        return (sse, grad_u, grad_v)

    start = (
        jnp.zeros((), jnp.float32),
        jnp.zeros(user_b.shape, jnp.float32),
        jnp.zeros(item_b.shape, jnp.float32),
    )
    return lax.fori_loop(0, slots, one, start)


def local(
    ratings,
    tile_index,
    tile_count,
    side_features,
    user_factors,
    item_factors,
    prior_weights,
    user_noise,
    item_noise,
):
    devices = lax.axis_size(USER)
    own = lax.axis_index(USER)
    tile = ratings.shape[-1]
    strata = ratings.shape[1]
    rows_dev = user_factors.shape[0]
    feat_rows = prior_weights.shape[0] // devices
    rate = rate_scale / (rows_dev * devices)
    noise_scale = math.sqrt(2.0 * step_size)
    users = user_factors
    items = item_factors
    weights = prior_weights
    final_rows = weights
    for stratum in range(strata):
        mean = jnp.dot(
            side_features, weights.astype(jnp.bfloat16), preferred_element_type=jnp.float32
        )
        offset = (users - mean).astype(jnp.bfloat16)
        user_b = users.astype(jnp.bfloat16)
        item_b = items.astype(jnp.bfloat16)
        count = tile_count[0, stratum]
        sse, grad_u, grad_v = tile_pass(
            ratings[0, stratum], tile_index[0, stratum], count, user_b, item_b
        )
        count_here = count.astype(jnp.float32) * float(tile * tile)
        total_sse, total_count = packed_total(
            (sse, count_here), (("user_0", "user_1"), ("user_2", "user_3"))
        )
        precision = (1.0 + total_count / 2.0) / (1.0 + total_sse / 2.0)
        last = stratum + 1 == strata
        grad_w = lax.dot_general(
            side_features, offset, (((0,), (0,)), ((), ())), preferred_element_type=jnp.float32
        )
        total = total_of(grad_w, (("user_0", "user_1"), ("user_2", "user_3")))
        full_new = weights + rate * (prior_prec * total - weight_decay * weights)
        if last:
            final_rows = lax.dynamic_slice_in_dim(full_new, own * feat_rows, feat_rows, 0)
        else:
            weights = full_new
        new_users = (
            users
            + step_size * (precision * grad_u - prior_prec * (users - mean))
            + noise_scale * user_noise[stratum].astype(jnp.float32)
        )
        new_items = (
            items
            + step_size * (precision * grad_v - item_prec * items)
            + noise_scale * item_noise[stratum].astype(jnp.float32)
        )
        users = new_users
        if last:
            items = new_items
        else:
            items = shifted(new_items, USER, 1)
    return (users, items, final_rows)


def solution(mesh):
    finer = Mesh(mesh.devices.reshape(16, 4, 4, 2), ("user_0", "user_1", "user_2", "user_3"))
    return jax.shard_map(
        local,
        mesh=finer,
        in_specs=(
            P(USER, None, None, None, None),
            P(USER, None, None),
            P(USER, None),
            P(USER, None),
            P(USER, None),
            P(USER, None),
            P(),
            P(None, USER, None),
            P(None, USER, None),
        ),
        out_specs=(P(USER, None), P(USER, None), P(USER, None)),
        check_vma=False,
    )
```

profile of v0, /device:TPU:1, one launch (start us, length us, event | category | flops | bytes accessed | tf_op | source)
XLA Modules:
  0.0 498.8 jit_solution(4620931035502280243)
XLA Ops:
  5.6 34.7 %while.57 = (s32[]{:T(128)}, f32[]{:T(128)}, f32[384,256]{1,0:T(8,128)S(1)}, f32[384,256]{1,0:T(8,128)S(1)}, bf16[6,128,128]{2,1,0:T(8,128)(2,1)}, /*index=5*/s3...) while((s32[]{:T(128)}, f32[]{:T(128)}, ...), condition=%wide.region_2.3_spmd, body=%wide.region_0.2_spmd.sunk | while | flops 25329688 | bytes 917950 | solution.py:130
  40.4 13.8 %all_to_all.98 = f32[8,1,2]{2,1,0:T(1,128)S(1)} all-to-all(f32[8,1,2]{2,1,0:T(1,128)S(1)} %broadcast_in_dim.24), channel_id=1, replica_groups=mesh['user_0'=16,'user_1'=4,'user_2'=4,'user_3'=2] {'user_2','user_3'}, dimensions={0} | all-to-all | bytes 128 | tf_op jit(solution)/shard_map/all_to_all | solution.py:21
  54.3 28.1 %all_to_all.99 = f32[64,1,2]{2,1,0:T(1,128)S(1)} all-to-all(f32[64,1,2]{2,1,0:T(1,128)S(1)} %broadcast_in_dim.25), channel_id=1, replica_groups=mesh['user_0'=16,'user_1'=4,'user_2'=4,'user_3'=2] {'user_0','user_1'}, dimensions={0} | all-to-all | bytes 1024 | tf_op jit(solution)/shard_map/all_to_all | solution.py:21
  90.6 19.5 %all_to_all.100 = f32[8,64,2,256]{3,2,1,0:T(2,128)S(1)} all-to-all(f32[8,64,2,256]{3,2,1,0:T(2,128)S(1)} %copy.54), channel_id=1, replica_groups=mesh['user_0'=16,'user_1'=4,'user_2'=4,'user_3'=2] {'user_2','user_3'}, dimensions={0} | all-to-all | bytes 2097152 | tf_op jit(solution)/shard_map/all_to_all | solution.py:70
  110.5 19.2 %all_to_all.101 = f32[64,2,256]{2,1,0:T(2,128)S(1)} all-to-all(f32[64,2,256]{2,1,0:T(2,128)S(1)} %reduce_sum.160), channel_id=1, replica_groups=mesh['user_0'=16,'user_1'=4,'user_2'=4,'user_3'=2] {'user_0','user_1'}, dimensions={0} | all-to-all | bytes 262144 | tf_op jit(solution)/shard_map/all_to_all | solution.py:78
  129.9 21.0 %all_to_all.96 = f32[64,2,256]{2,1,0:T(2,128)S(1)} all-to-all(f32[64,2,256]{2,1,0:T(2,128)S(1)} %broadcast_in_dim.28), channel_id=1, replica_groups=mesh['user_0'=16,'user_1'=4,'user_2'=4,'user_3'=2] {'user_0','user_1'}, dimensions={0} | all-to-all | bytes 262144 | tf_op jit(solution)/shard_map/all_to_all | solution.py:21
  152.1 6.6 %all-to-all-start.7 = ((f32[8,64,2,256]{3,2,1,0:T(2,128)}), f32[8,64,2,256]{3,2,1,0:T(2,128)S(1)}, u32[]{:S(2)}, u32[]{:S(2)}) async-start(f32[8,64,2,256]{3,2,1,0:T(2,128)} %broadcast_in_dim.29), calls=%async_computation.7 | async-start | bytes 2097152 | tf_op jit(solution)/shard_map/all_to_all | solution.py:21
  164.7 10.3 %collective-permute-done = f32[384,256]{1,0:T(8,128)S(1)} collective-permute-done((f32[384,256]{1,0:T(8,128)}, f32[384,256]{1,0:T(8,128)S(1)}, u32[]{:S(2)}, u32[]{:S(2)}) %collective-permute-start) | collective-permute-done | bytes 393248 | tf_op jit(solution)/shard_map/ppermute | solution.py:91
  192.4 6.5 %all-to-all-start.10 = ((f32[8,64,2,256]{3,2,1,0:T(2,128)}), f32[8,64,2,256]{3,2,1,0:T(2,128)}, u32[]{:S(2)}, u32[]{:S(2)}) async-start(f32[8,64,2,256]{3,2,1,0:T(2,128)} %copy.61), calls=%async_computation.10 | async-start | bytes 2097152 | tf_op jit(solution)/shard_map/all_to_all | solution.py:70
  199.7 45.6 %while.58 = (s32[]{:T(128)}, f32[]{:T(128)}, f32[384,256]{1,0:T(8,128)S(1)}, f32[384,256]{1,0:T(8,128)}, bf16[6,128,128]{2,1,0:T(8,128)(2,1)}, /*index=5*/s32[6]...) while((s32[]{:T(128)}, f32[]{:T(128)}, ...), condition=%wide.region_7.8_spmd, body=%wide.region_5.7_spmd.sunk | while | flops 25329688 | bytes 917950 | solution.py:130
  260.2 15.5 %all-to-all-done.11 = f32[64,2,256]{2,1,0:T(2,128)S(1)} async-done(((f32[64,2,256]{2,1,0:T(2,128)}), f32[64,2,256]{2,1,0:T(2,128)S(1)}, u32[]{:S(2)}, u32[]{:S(2)}) %all-to-all-start.11) | async-done | bytes 131104 | tf_op jit(solution)/shard_map/all_to_all | solution.py:78
  276.3 5.9 %all-to-all-start.3 = ((f32[64,1,2]{2,1,0:T(1,128)}), f32[64,1,2]{2,1,0:T(1,128)S(1)}, u32[]{:S(2)}, u32[]{:S(2)}) async-start(f32[64,1,2]{2,1,0:T(1,128)} %broadcast_in_dim.27), calls=%async_computation.3 | async-start | bytes 65536 | tf_op jit(solution)/shard_map/all_to_all | solution.py:21
  282.3 13.6 %all-to-all-done.3 = f32[64,1,2]{2,1,0:T(1,128)S(1)} async-done(((f32[64,1,2]{2,1,0:T(1,128)}), f32[64,1,2]{2,1,0:T(1,128)S(1)}, u32[]{:S(2)}, u32[]{:S(2)}) %all-to-all-start.3) | async-done | bytes 544 | tf_op jit(solution)/shard_map/all_to_all | solution.py:21
  303.1 13.2 %all-to-all-done.12 = f32[64,2,256]{2,1,0:T(2,128)S(1)} async-done(((f32[64,2,256]{2,1,0:T(2,128)}), f32[64,2,256]{2,1,0:T(2,128)S(1)}, u32[]{:S(2)}, u32[]{:S(2)}) %all-to-all-start.12) | async-done | bytes 131104 | tf_op jit(solution)/shard_map/all_to_all | solution.py:21
  317.6 8.3 %all-to-all-start.13 = ((f32[8,64,2,256]{3,2,1,0:T(2,128)}), f32[8,64,2,256]{3,2,1,0:T(2,128)}, u32[]{:S(2)}, u32[]{:S(2)}) async-start(f32[8,64,2,256]{3,2,1,0:T(2,128)} %broadcast_in_dim.33), calls=%async_computation.13 | async-start | bytes 2097152 | tf_op jit(solution)/shard_map/all_to_all | solution.py:21
  332.0 10.2 %collective-permute-done.1 = f32[384,256]{1,0:T(8,128)} collective-permute-done((f32[384,256]{1,0:T(8,128)}, f32[384,256]{1,0:T(8,128)}, u32[]{:S(2)}, u32[]{:S(2)}) %collective-permute-start.1) | collective-permute-done | bytes 393248 | tf_op jit(solution)/shard_map/ppermute | solution.py:91
  358.2 8.7 %all-to-all-start.14 = ((f32[8,64,2,256]{3,2,1,0:T(2,128)}), f32[8,64,2,256]{3,2,1,0:T(2,128)S(1)}, u32[]{:S(2)}, u32[]{:S(2)}) async-start(f32[8,64,2,256]{3,2,1,0:T(2,128)} %copy.66), calls=%async_computation.14 | async-start | bytes 2097152 | tf_op jit(solution)/shard_map/all_to_all | solution.py:70
  367.9 34.2 %while.59 = (s32[]{:T(128)}, f32[]{:T(128)}, f32[384,256]{1,0:T(8,128)S(1)}, f32[384,256]{1,0:T(8,128)S(1)}, bf16[6,128,128]{2,1,0:T(8,128)(2,1)}, /*index=5*/s3...) while((s32[]{:T(128)}, f32[]{:T(128)}, ...), condition=%wide.region_14.15_spmd, body=%wide.region_12.14_spmd.sunk | while | flops 25329688 | bytes 917950 | solution.py:130
  416.9 15.5 %all-to-all-done.15 = f32[64,2,256]{2,1,0:T(2,128)S(1)} async-done(((f32[64,2,256]{2,1,0:T(2,128)}), f32[64,2,256]{2,1,0:T(2,128)S(1)}, u32[]{:S(2)}, u32[]{:S(2)}) %all-to-all-start.15) | async-done | bytes 131104 | tf_op jit(solution)/shard_map/all_to_all | solution.py:78
  433.0 5.9 %all-to-all-start.9 = ((f32[64,1,2]{2,1,0:T(1,128)}), f32[64,1,2]{2,1,0:T(1,128)S(1)}, u32[]{:S(2)}, u32[]{:S(2)}) async-start(f32[64,1,2]{2,1,0:T(1,128)} %broadcast_in_dim.31), calls=%async_computation.9 | async-start | bytes 65536 | tf_op jit(solution)/shard_map/all_to_all | solution.py:21
  439.0 13.3 %all-to-all-done.9 = f32[64,1,2]{2,1,0:T(1,128)S(1)} async-done(((f32[64,1,2]{2,1,0:T(1,128)}), f32[64,1,2]{2,1,0:T(1,128)S(1)}, u32[]{:S(2)}, u32[]{:S(2)}) %all-to-all-start.9) | async-done | bytes 544 | tf_op jit(solution)/shard_map/all_to_all | solution.py:21
  452.3 19.2 %all_to_all.97 = f32[64,2,256]{2,1,0:T(2,128)S(1)} all-to-all(f32[64,2,256]{2,1,0:T(2,128)S(1)} %broadcast_in_dim.34), channel_id=1, replica_groups=mesh['user_0'=16,'user_1'=4,'user_2'=4,'user_3'=2] {'user_0','user_1'}, dimensions={0} | all-to-all | bytes 262144 | tf_op jit(solution)/shard_map/all_to_all | solution.py:21
  472.8 7.9 %all-to-all-start.17 = ((f32[8,64,2,256]{3,2,1,0:T(2,128)}), f32[8,64,2,256]{3,2,1,0:T(2,128)S(1)}, u32[]{:S(2)}, u32[]{:S(2)}) async-start(f32[8,64,2,256]{3,2,1,0:T(2,128)} %broadcast_in_dim.35), calls=%async_computation.17 | async-start | bytes 2097152 | tf_op jit(solution)/shard_map/all_to_all | solution.py:21
  485.0 10.6 %all-to-all-done.17 = f32[8,64,2,256]{3,2,1,0:T(2,128)S(1)} async-done(((f32[8,64,2,256]{3,2,1,0:T(2,128)}), f32[8,64,2,256]{3,2,1,0:T(2,128)S(1)}, u32[]{:S(2)}, u32[]{:S(2)}) %all-to-all-start.17) | async-done | bytes 1048608 | tf_op jit(solution)/shard_map/all_to_all | solution.py:21
  (186 shorter events, 160.8 us)
Async XLA Ops:
  0.6 83.8 %copy-start = (bf16[384,1024]{1,0:T(8,128)(2,1)S(1)}, bf16[384,1024]{1,0:T(8,128)(2,1)}, u32[]{:S(2)}) copy-start(bf16[384,1024]{1,0:T(8,128)(2,1)} %param.18) | copy-start | bytes 2359300
  0.6 2.0 copy-start.13
  0.7 2.0 copy-start.11
  2.7 1.0 copy-start.9
  5.6 78.8 %copy-start.1 = (f32[1024,256]{1,0:T(8,128)S(1)}, f32[1024,256]{1,0:T(8,128)}, u32[]{:S(2)}) copy-start(f32[1024,256]{1,0:T(8,128)} %param.21) | copy-start | bytes 3145732
  152.1 25.5 %all-to-all-start.7 = ((f32[8,64,2,256]{3,2,1,0:T(2,128)}), f32[8,64,2,256]{3,2,1,0:T(2,128)S(1)}, u32[]{:S(2)}, u32[]{:S(2)}) async-start(f32[8,64,2,256]{3,2,1,0:T(2,128)} %broadcast_in_dim.29), calls=%async_computation.7 | async-start | bytes 2097152 | tf_op jit(solution)/shard_map/all_to_all | solution.py:21
  160.6 14.4 %collective-permute-start = (f32[384,256]{1,0:T(8,128)}, f32[384,256]{1,0:T(8,128)S(1)}, u32[]{:S(2)}, u32[]{:S(2)}) collective-permute-start(f32[384,256]{1,0:T(8,128)} %bitcast_add_fusion.4), channel_id=1, source_target_pairs={{0,1},{1,2},{2,3},{3,4},{4,5},{5,6},{6,7},{7,8},{8,9},{9,10},{10,1... | collective-permute-start | bytes 1179656 | tf_op jit(solution)/shard_map/ppermute | solution.py:91
  175.0 3.1 copy-start.10
  179.7 2.0 copy-start.4
  192.4 53.0 %all-to-all-start.10 = ((f32[8,64,2,256]{3,2,1,0:T(2,128)}), f32[8,64,2,256]{3,2,1,0:T(2,128)}, u32[]{:S(2)}, u32[]{:S(2)}) async-start(f32[8,64,2,256]{3,2,1,0:T(2,128)} %copy.61), calls=%async_computation.10 | async-start | bytes 2097152 | tf_op jit(solution)/shard_map/all_to_all | solution.py:70
  246.0 9.4 %all-to-all-start.2 = ((f32[8,1,2]{2,1,0:T(1,128)}), f32[8,1,2]{2,1,0:T(1,128)S(1)}, u32[]{:S(2)}, u32[]{:S(2)}) async-start(f32[8,1,2]{2,1,0:T(1,128)} %broadcast_in_dim.26), calls=%async_computation.2 | async-start | bytes 8192 | tf_op jit(solution)/shard_map/all_to_all | solution.py:21
  255.4 20.3 %all-to-all-start.11 = ((f32[64,2,256]{2,1,0:T(2,128)}), f32[64,2,256]{2,1,0:T(2,128)S(1)}, u32[]{:S(2)}, u32[]{:S(2)}) async-start(f32[64,2,256]{2,1,0:T(2,128)} %reduce_sum.164), calls=%async_computation.11 | async-start | bytes 262144 | tf_op jit(solution)/shard_map/all_to_all | solution.py:78
  276.3 19.6 %all-to-all-start.3 = ((f32[64,1,2]{2,1,0:T(1,128)}), f32[64,1,2]{2,1,0:T(1,128)S(1)}, u32[]{:S(2)}, u32[]{:S(2)}) async-start(f32[64,1,2]{2,1,0:T(1,128)} %broadcast_in_dim.27), calls=%async_computation.3 | async-start | bytes 65536 | tf_op jit(solution)/shard_map/all_to_all | solution.py:21
  296.5 19.8 %all-to-all-start.12 = ((f32[64,2,256]{2,1,0:T(2,128)}), f32[64,2,256]{2,1,0:T(2,128)S(1)}, u32[]{:S(2)}, u32[]{:S(2)}) async-start(f32[64,2,256]{2,1,0:T(2,128)} %broadcast_in_dim.32), calls=%async_computation.12 | async-start | bytes 262144 | tf_op jit(solution)/shard_map/all_to_all | solution.py:21
  317.6 28.3 %all-to-all-start.13 = ((f32[8,64,2,256]{3,2,1,0:T(2,128)}), f32[8,64,2,256]{3,2,1,0:T(2,128)}, u32[]{:S(2)}, u32[]{:S(2)}) async-start(f32[8,64,2,256]{3,2,1,0:T(2,128)} %broadcast_in_dim.33), calls=%async_computation.13 | async-start | bytes 2097152 | tf_op jit(solution)/shard_map/all_to_all | solution.py:21
  327.9 14.3 %collective-permute-start.1 = (f32[384,256]{1,0:T(8,128)}, f32[384,256]{1,0:T(8,128)}, u32[]{:S(2)}, u32[]{:S(2)}) collective-permute-start(f32[384,256]{1,0:T(8,128)} %bitcast_add_fusion.2), channel_id=1, source_target_pairs={{0,1},{1,2},{2,3},{3,4},{4,5},{5,6},{6,7},{7,8},{8,9},{9,10},{10,1... | collective-permute-start | bytes 1179656 | tf_op jit(solution)/shard_map/ppermute | solution.py:91
  332.0 11.9 %copy-start.5 = (f32[384,256]{1,0:T(8,128)S(1)}, f32[384,256]{1,0:T(8,128)}, u32[]{:S(2)}) copy-start(f32[384,256]{1,0:T(8,128)} %get-tuple-element.744) | copy-start | bytes 1179652
  352.2 1.5 copy-start.6
  353.7 1.0 copy-start.2
  358.2 44.0 %all-to-all-start.14 = ((f32[8,64,2,256]{3,2,1,0:T(2,128)}), f32[8,64,2,256]{3,2,1,0:T(2,128)S(1)}, u32[]{:S(2)}, u32[]{:S(2)}) async-start(f32[8,64,2,256]{3,2,1,0:T(2,128)} %copy.66), calls=%async_computation.14 | async-start | bytes 2097152 | tf_op jit(solution)/shard_map/all_to_all | solution.py:70
  402.8 9.4 %all-to-all-start.8 = ((f32[8,1,2]{2,1,0:T(1,128)}), f32[8,1,2]{2,1,0:T(1,128)S(1)}, u32[]{:S(2)}, u32[]{:S(2)}) async-start(f32[8,1,2]{2,1,0:T(1,128)} %broadcast_in_dim.30), calls=%async_computation.8 | async-start | bytes 8192 | tf_op jit(solution)/shard_map/all_to_all | solution.py:21
  412.2 20.1 %all-to-all-start.15 = ((f32[64,2,256]{2,1,0:T(2,128)}), f32[64,2,256]{2,1,0:T(2,128)S(1)}, u32[]{:S(2)}, u32[]{:S(2)}) async-start(f32[64,2,256]{2,1,0:T(2,128)} %reduce_sum.166), calls=%async_computation.15 | async-start | bytes 262144 | tf_op jit(solution)/shard_map/all_to_all | solution.py:78
  433.0 19.3 %all-to-all-start.9 = ((f32[64,1,2]{2,1,0:T(1,128)}), f32[64,1,2]{2,1,0:T(1,128)S(1)}, u32[]{:S(2)}, u32[]{:S(2)}) async-start(f32[64,1,2]{2,1,0:T(1,128)} %broadcast_in_dim.31), calls=%async_computation.9 | async-start | bytes 65536 | tf_op jit(solution)/shard_map/all_to_all | solution.py:21
  472.8 22.9 %all-to-all-start.17 = ((f32[8,64,2,256]{3,2,1,0:T(2,128)}), f32[8,64,2,256]{3,2,1,0:T(2,128)S(1)}, u32[]{:S(2)}, u32[]{:S(2)}) async-start(f32[8,64,2,256]{3,2,1,0:T(2,128)} %broadcast_in_dim.35), calls=%async_computation.17 | async-start | bytes 2097152 | tf_op jit(solution)/shard_map/all_to_all | solution.py:21
  (4 other events, 3.1 us)
where the time goes:
time: 503 us; the launch traced here: 499 us
  blocking collectives  121 us (24%)
  waiting for transfers between devices  111 us (22%)
  starting transfers between devices  80.5 us (16%)
  loops' own time  58.5 us (12%)
  local copies, waits for them, and re-layouts  51.3 us (10%)
  matrix products  50.3 us (10%)
  other arithmetic  20.2 us (4%)
  between operations  6.74 us (1%)
    all_to_all x4, blocking collectives, from_everyone(): lax.all_to_all(jnp.broadcast_to(array[None], (devices, *array.shape)), ax...  82 us
    all_to_all x8, waiting for transfers between devices, from_everyone(): lax.all_to_all(jnp.broadcast_to(array[None], (devices, *array.shape)), ax...  59.1 us
    another operation x3, loops' own time, tile_pass(): return lax.fori_loop(0, slots, one, start)  58.5 us
    all_to_all x8, starting transfers between devices, from_everyone(): lax.all_to_all(jnp.broadcast_to(array[None], (devices, *array.shape)), ax...  48.8 us
    all_to_all x2, waiting for transfers between devices, sum_by_axis(): lax.all_to_all(nearer, far, split_axis=0, concat_axis=0, tiled=True)  31 us
    dot_general x18, matrix products, one(): lax.dot_general(user_tile, item_tile, (((1,), (1,)), ((), ())), preferred...  28.9 us
    ppermute x2, waiting for transfers between devices, shifted(): lax.ppermute(array, axis, [(i, (i + by) % devices) for i in range(devices)])  20.5 us
    all_to_all x1, blocking collectives, sum_at_owner(): lax.all_to_all(in_blocks(array, dim, devices), axis, 0, 0, tiled=True)  19.5 us
  transfers between devices with their start and end apart: 14, of which 11 were waited for; matrix products, arithmetic and copies ran while one was open for 11% of the time, Pallas kernels for 0%

commit v1 on v0

v1 whole, which is shorter than its diff:
```python
import functools
import math

import jax
import jax.numpy as jnp
from jax import lax
from jax.experimental import pallas as pl
from jax.experimental.pallas import tpu as pltpu
from jax.sharding import Mesh
from jax.sharding import PartitionSpec as P

USER = ("user_0", "user_1", "user_2", "user_3")
MESH = pl.DeviceIdType.MESH
F32 = jnp.float32
BF16 = jnp.bfloat16

step_size = 0.01
prior_prec = 8.0
item_prec = 1.0
weight_decay = 1.0
rate_scale = 0.04


def nt(a, b):
    return lax.dot_general(a, b, (((1,), (1,)), ((), ())), preferred_element_type=F32)


def tn(a, b):
    return lax.dot_general(a, b, (((0,), (0,)), ((), ())), preferred_element_type=F32)


def kernel(
    dims,
    index_ref, count_ref, ratings_hbm, feat_hbm, users_hbm, items_hbm, weights_hbm, unoise_hbm, inoise_hbm,
    users_out, items_out, weights_out,
    ratings, feat, featT, users, items, new_items, w0, wb, unoise, inoise, mean, off, err_b, grad_u, grad_v,
    g_send, g_sum, core_in, plane_in, z_out, z_in, w_own, wz, wfull, pay, sse_plane, pay2, sse_z, fin, wout,
    load, store, core_s, core_r, prs_s, prs_r, zrs_s, zrs_r, zag_s, zag_r, pag_s, pag_r, fwd_s, fwd_r,
    sp_s, sp_r, sz_s, sz_r, sh_s, sh_r, fin_s, fin_r,
):
    NZ, NX, NY, strata, slots, tile, rows, featn, rank = dims
    NP = NX * NY
    half = rank // 2
    grid = rows // tile
    T2 = NZ // 2
    rate = rate_scale / (rows * NZ * NP * 2)
    noise_scale = math.sqrt(2.0 * step_size)

    z = lax.axis_index("user_0")
    x = lax.axis_index("user_1")
    y = lax.axis_index("user_2")
    c = lax.axis_index("user_3")
    p = x * NY + y
    par = lax.rem(y, 2)
    pp = p // 2
    owner = lax.rem(z + y, 2) == 0
    partner = (z, x, y, 1 - c)

    def plane_peer(i):
        return lax.rem(x + i // NY, NX), lax.rem(y + lax.rem(i, NY), NY)

    def device_of(idx):
        cc = lax.rem(idx, 2)
        k = idx // 2
        yy = lax.rem(k, NY)
        k = k // NY
        return (k // NX, lax.rem(k, NX), yy, cc)

    total = NZ * NP * 2
    me = (z * NP + p) * 2 + c
    nxt = device_of(lax.rem(me + 1, total))
    prv = device_of(lax.rem(me + total - 1, total))

    def bytes_wait(ref, sem):
        pltpu.make_async_copy(ref, ref, sem).wait()

    def remote(src, dst, s_sem, r_sem, dev):
        return pltpu.make_async_remote_copy(src_ref=src, dst_ref=dst, send_sem=s_sem, recv_sem=r_sem,
                                            device_id=dev, device_id_type=MESH)

    pairs = ((feat_hbm, feat), (weights_hbm, w0), (users_hbm, users), (items_hbm, items.at[0]),
             (ratings_hbm.at[0], ratings), (unoise_hbm, unoise), (inoise_hbm, inoise))
    loads = [pltpu.make_async_copy(a, b, load.at[i]) for i, (a, b) in enumerate(pairs)]
    for cp in loads:
        cp.start()

    barrier = pltpu.get_barrier_semaphore()

    def hello(dev):
        pl.semaphore_signal(barrier, inc=1, device_id=dev, device_id_type=MESH)

    def hello_plane(i, _):
        xx, yy = plane_peer(i)
        hello((z, xx, yy, c))
        hello((z, xx, yy, 1 - c))
        return 0

    def hello_z(i, _):
        hello((lax.rem(z + i, NZ), x, y, c))
        return 0

    hello(partner)
    hello(nxt)
    hello(prv)
    lax.fori_loop(1, NP, hello_plane, 0)
    lax.fori_loop(1, NZ, hello_z, 0)

    def tile_pass(s):
        ub = users[...].astype(BF16)
        hb = items[s].astype(BF16)
        count = count_ref[0, s]
        sse = jnp.zeros((1, tile), F32)
        for r in range(grid):
            pred = nt(ub[r * tile:(r + 1) * tile], hb)
            parts = []
            for col in range(grid):
                k = r * grid + col
                slot = jnp.int32(0)
                live = jnp.float32(0.0)
                for t in range(slots):
                    hit = index_ref[0, s, t] == k
                    slot = jnp.where(hit, jnp.int32(t), slot)
                    live = jnp.where(jnp.logical_and(hit, t < count), jnp.float32(1.0), live)
                e = live * (ratings[s, slot].astype(F32) - pred[:, col * tile:(col + 1) * tile])
                sse = sse + jnp.sum(e * e, axis=0, keepdims=True)
                parts.append(e.astype(BF16))
            row = jnp.concatenate(parts, axis=1)
            err_b[r * tile:(r + 1) * tile, :] = row
            grad_u[r * tile:(r + 1) * tile, :] = jnp.dot(row, hb, preferred_element_type=F32)
        grad_v[...] = tn(err_b[...], ub)
        pay[s, 0:1, :] = sse
        pay[s, 1:2, :] = jnp.broadcast_to(count.astype(F32) * float(tile * tile) / float(tile), (1, tile))

    def sse_plane_send(s):
        slot = p * 2 + c
        dst = sse_plane.at[s, slot]
        remote(pay.at[s], dst, sp_s.at[s], sp_r.at[s], partner).start()

        def body(i, _):
            xx, yy = plane_peer(i)
            remote(pay.at[s], dst, sp_s.at[s], sp_r.at[s], (z, xx, yy, c)).start()
            remote(pay.at[s], dst, sp_s.at[s], sp_r.at[s], (z, xx, yy, 1 - c)).start()
            return 0

        lax.fori_loop(1, NP, body, 0)
        sse_plane[s, slot] = pay[s]

    def sse_z_send(s):
        bytes_wait(sse_plane.at[s, pl.ds(0, 2 * NP - 1)], sp_r.at[s])
        tot = jnp.sum(sse_plane[s], axis=0)
        pay2[s] = tot
        sse_z[s, z] = tot

        def body(i, _):
            remote(pay2.at[s], sse_z.at[s, z], sz_s.at[s], sz_r.at[s], (lax.rem(z + i, NZ), x, y, c)).start()
            return 0

        lax.fori_loop(1, NZ, body, 0)

    def update(s, dst_items):
        bytes_wait(sse_z.at[s, pl.ds(0, NZ - 1)], sz_r.at[s])
        tot = jnp.sum(sse_z[s], axis=0)
        sums = jnp.sum(tot, axis=1, keepdims=True)
        precision = (1.0 + sums[1:2, :] / 2.0) / (1.0 + sums[0:1, :] / 2.0)
        pr = jnp.broadcast_to(precision, (1, rank))
        if s == 0:
            loads[6].wait()
            loads[5].wait()
        h = items[s]
        dst_items[...] = (h + step_size * (pr * grad_v[...] - item_prec * h)
                          + noise_scale * inoise[s].astype(F32))
        if s + 1 < strata:
            remote(new_items.at[s], items.at[s + 1], sh_s.at[s], sh_r.at[s], nxt).start()
        u = users[...]
        users[...] = (u + step_size * (pr * grad_u[...] - prior_prec * (u - mean[...]))
                      + noise_scale * unoise[s].astype(F32))

    for s in range(strata):
        last = s + 1 == strata
        if s == 0:
            loads[0].wait()
            loads[1].wait()
            wb[...] = w0[...].astype(BF16)
            for i in range(rows // 128):
                featT[:, i * 128:(i + 1) * 128] = feat[i * 128:(i + 1) * 128, :].T
            t_own = z * (NP // 2) + pp
            own8 = w0[pl.ds(pl.multiple_of(t_own * 8, 8), 8), :]
            w_own[...] = jnp.where(c == 0, own8[:, :half], own8[:, half:])
        mean[...] = jnp.dot(feat[...], wb[...], preferred_element_type=F32)
        if s == 0:
            loads[2].wait()
        o = (users[...] - mean[...]).astype(BF16)
        off[0] = o[:, :half]
        off[1] = o[:, half:]
        if s > 0:
            bytes_wait(g_send, core_s.at[s - 1])
        g_send[...] = jnp.dot(featT[...], off[1 - c], preferred_element_type=F32).reshape(g_send.shape)
        if s == 0:
            pl.semaphore_wait(barrier, 2 * (NP - 1) + NZ - 1 + 3)
        remote(g_send, core_in.at[s], core_s.at[s], core_r.at[s], partner).start()
        if s > 0:
            bytes_wait(plane_in.at[s, pl.ds(0, NP - 1)], prs_s.at[s - 1])
        g_sum[...] = jnp.dot(featT[...], off[c], preferred_element_type=F32).reshape(g_sum.shape)
        if s == 0:
            loads[3].wait()
            loads[4].wait()
            tile_pass(0)
            sse_plane_send(0)
        bytes_wait(core_in.at[s], core_r.at[s])
        g_sum[...] = g_sum[...] + core_in[s]

        def plane_send(i, _):
            xx, yy = plane_peer(NP - i)
            q = xx * NY + yy
            remote(g_sum.at[:, lax.rem(q, 2), q // 2], plane_in.at[s, p], prs_s.at[s], prs_r.at[s], (z, xx, yy, c)).start()
            return 0

        lax.fori_loop(1, NP, plane_send, 0)
        plane_in[s, p] = g_sum[:, par, pp]
        if s > 0:
            sse_z_send(s)
        bytes_wait(plane_in.at[s, pl.ds(0, NP - 1)], prs_r.at[s])
        acc = plane_in[s, 0]
        for q in range(1, NP):
            acc = acc + plane_in[s, q]
        if s > 0:
            @pl.when(owner)
            def _():
                bytes_wait(z_out.at[pl.ds(0, T2 - 1)], zrs_s.at[s - 1])

            @pl.when(jnp.logical_not(owner))
            def _():
                bytes_wait(z_out, zrs_s.at[s - 1])
        z_out[...] = acc
        shift = lax.rem(z + y, 2)

        def z_send(i, _):
            zz = lax.rem(z + shift + 2 * i, NZ)

            @pl.when(zz != z)
            def _():
                remote(z_out.at[zz // 2], z_in.at[s, z], zrs_s.at[s], zrs_r.at[s], (zz, x, y, c)).start()

            return 0

        lax.fori_loop(0, T2, z_send, 0)
        if s == 0:
            sse_z_send(0)

        @pl.when(owner)
        def _():
            z_in[s, z] = z_out[z // 2]
            bytes_wait(z_in.at[s, pl.ds(0, NZ - 1)], zrs_r.at[s])
            g = z_in[s, 0]
            for k in range(1, NZ):
                g = g + z_in[s, k]
            w = w_own[...]
            w = w + rate * (prior_prec * g - weight_decay * w)
            w_own[...] = w
            if last:
                fin[c] = w
                for n, dev in enumerate((partner, (z, x, y + 1 - 2 * par, c), (z, x, y + 1 - 2 * par, 1 - c))):
                    remote(w_own, fin.at[c], fin_s.at[n], fin_r.at[c], dev).start()
            else:
                wz[s, z // 2] = w

                def ag_send(i, _):
                    remote(wz.at[s, z // 2], wz.at[s, z // 2], zag_s.at[s], zag_r.at[s], (lax.rem(z + i, NZ), x, y, c)).start()
                    return 0

                lax.fori_loop(1, NZ, ag_send, 0)

        if last:
            update(s, new_items.at[s])
            st = [pltpu.make_async_copy(users, users_out, store.at[0]),
                  pltpu.make_async_copy(new_items.at[s], items_out, store.at[1])]
            for cp in st:
                cp.start()

            @pl.when(owner)
            def _():
                bytes_wait(fin.at[0], fin_r.at[1 - c])

            @pl.when(jnp.logical_not(owner))
            def _():
                bytes_wait(fin.at[0], fin_r.at[0])
                bytes_wait(fin.at[1], fin_r.at[1])

            r0 = par * 4 + c * 2
            for h in range(2):
                t8 = fin[h]
                o2 = t8[0:2]
                for k in range(1, 4):
                    o2 = jnp.where(r0 == 2 * k, t8[2 * k:2 * k + 2], o2)
                wout[:, h * half:(h + 1) * half] = o2
            cp = pltpu.make_async_copy(wout, weights_out, store.at[2])
            cp.start()
            for d in (*st, cp):
                d.wait()
        else:
            update(s, new_items.at[s])

            @pl.when(owner)
            def _():
                bytes_wait(wz.at[s, pl.ds(0, T2 - 1)], zag_r.at[s])

            @pl.when(jnp.logical_not(owner))
            def _():
                bytes_wait(wz.at[s], zag_r.at[s])

            def pag_send(i, _):
                xx, yy = plane_peer(NP - i)
                remote(wz.at[s], wfull.at[s, c, :, par, pp], pag_s.at[s], pag_r.at[s, p], (z, xx, yy, c)).start()
                return 0

            lax.fori_loop(1, NP, pag_send, 0)
            remote(wz.at[s], wfull.at[s, c, :, par, pp], fwd_s.at[s], fwd_r.at[s], partner).start()
            wfull[s, c, :, par, pp] = wz[s]
            bytes_wait(items.at[s + 1], sh_r.at[s])
            bytes_wait(new_items.at[s], sh_s.at[s])
            tile_pass(s + 1)
            sse_plane_send(s + 1)

            def forward(i, _):
                xx, yy = plane_peer(i)
                q = xx * NY + yy
                piece = wfull.at[s, c, :, lax.rem(q, 2), q // 2]
                bytes_wait(piece, pag_r.at[s, q])
                remote(piece, piece, fwd_s.at[s], fwd_r.at[s], partner).start()
                return 0

            lax.fori_loop(1, NP, forward, 0)
            bytes_wait(wfull.at[s, 1 - c], fwd_r.at[s])
            wb[:, :half] = wfull[s, 0].reshape(featn, half).astype(BF16)
            wb[:, half:] = wfull[s, 1].reshape(featn, half).astype(BF16)

    e = strata - 1
    bytes_wait(g_send, core_s.at[e])
    bytes_wait(plane_in.at[e, pl.ds(0, NP - 1)], prs_s.at[e])

    @pl.when(owner)
    def _():
        bytes_wait(z_out.at[pl.ds(0, T2 - 1)], zrs_s.at[e])
        for s in range(e):
            bytes_wait(z_in.at[s, pl.ds(0, NZ - 1)], zag_s.at[s])
        bytes_wait(core_in.at[e, 0, 0, pl.ds(0, 1)], fin_s.at[0])
        bytes_wait(core_in.at[e, 0, 0, pl.ds(0, 1)], fin_s.at[1])
        bytes_wait(core_in.at[e, 0, 0, pl.ds(0, 1)], fin_s.at[2])

    @pl.when(jnp.logical_not(owner))
    def _():
        bytes_wait(z_out, zrs_s.at[e])

    for s in range(strata):
        bytes_wait(sse_plane.at[s, pl.ds(0, 2 * NP - 1)], sp_s.at[s])
        bytes_wait(sse_z.at[s, pl.ds(0, NZ - 1)], sz_s.at[s])
        if s < e:
            bytes_wait(plane_in.at[s, pl.ds(0, NP - 1)], pag_s.at[s])
            bytes_wait(wfull.at[s, c], fwd_s.at[s])


def local(ratings, tile_index, tile_count, side, users, items, weights, unoise, inoise):
    nz, nx, ny = (lax.axis_size(a) for a in USER[:3])
    strata, slots, tile = ratings.shape[1:4]
    rows, rank = users.shape
    featn = side.shape[1]
    npl, t2, half = nx * ny, nz // 2, rank // 2
    dims = (nz, nx, ny, strata, slots, tile, rows, featn, rank)
    g_shape = (t2, 2, npl // 2, 8, half)
    V, D = pltpu.VMEM, pltpu.SemaphoreType.DMA
    data = [
        V((strata, slots, tile, tile), BF16),
        V((rows, featn), BF16),
        V((featn, rows), BF16),
        V((rows, rank), F32),
        V((strata, rows, rank), F32),
        V((strata, rows, rank), F32),
        V((featn, rank), F32),
        V((featn, rank), BF16),
        V((strata, rows, rank), BF16),
        V((strata, rows, rank), BF16),
        V((rows, rank), F32),
        V((2, rows, half), BF16),
        V((rows, rows), BF16),
        V((rows, rank), F32),
        V((rows, rank), F32),
        V(g_shape, F32),
        V(g_shape, F32),
        V((strata, *g_shape), F32),
        V((strata, npl, t2, 8, half), F32),
        V((t2, 8, half), F32),
        V((strata, nz, 8, half), F32),
        V((8, half), F32),
        V((strata - 1, t2, 8, half), F32),
        V((strata - 1, 2, *g_shape), F32),
        V((strata, 2, tile), F32),
        V((strata, 2 * npl, 2, tile), F32),
        V((strata, 2, tile), F32),
        V((strata, nz, 2, tile), F32),
        V((2, 8, half), F32),
        V((2, rank), F32),
    ]
    sems = [
        D((7,)), D((3,)),
        D((strata,)), D((strata,)),
        D((strata,)), D((strata,)),
        D((strata,)), D((strata,)),
        D((strata,)), D((strata,)),
        D((strata,)), D((strata, npl)),
        D((strata,)), D((strata,)),
        D((strata,)), D((strata,)),
        D((strata,)), D((strata,)),
        D((strata,)), D((strata,)),
        D((3,)), D((2,)),
    ]
    any_ = pl.BlockSpec(memory_space=pl.ANY)
    smem = pl.BlockSpec(memory_space=pltpu.SMEM)
    return pl.pallas_call(
        functools.partial(kernel, dims),
        out_shape=(
            jax.ShapeDtypeStruct((rows, rank), F32),
            jax.ShapeDtypeStruct((rows, rank), F32),
            jax.ShapeDtypeStruct((2, rank), F32),
        ),
        in_specs=[smem, smem] + [any_] * 7,
        out_specs=(any_, any_, any_),
        scratch_shapes=data + sems,
        compiler_params=pltpu.CompilerParams(collective_id=0, has_side_effects=True),
        name="sweep",
    )(tile_index, tile_count, ratings, side, users, items, weights, unoise, inoise)


def finer_of(mesh):
    return Mesh(mesh.devices.reshape(16, 4, 4, 2), USER)


def solution(mesh):
    return over(finer_of(mesh))


def over(finer):
    return jax.shard_map(
        local,
        mesh=finer,
        in_specs=(
            P(USER, None, None, None, None),
            P(USER, None, None),
            P(USER, None),
            P(USER, None),
            P(USER, None),
            P(USER, None),
            P(),
            P(None, USER, None),
            P(None, USER, None),
        ),
        out_specs=(P(USER, None), P(USER, None), P(USER, None)),
        check_vma=False,
    )
```

time: 503 us -> 112 us (0.22)
  blocking collectives: 121 us -> 0 us
  waiting for transfers between devices: 111 us -> 0 us
  Pallas kernels: 0 us -> 106 us
  starting transfers between devices: 80.5 us -> 0 us
  loops' own time: 58.5 us -> 0 us
  matrix products: 50.3 us -> 0 us
  local copies, waits for them, and re-layouts: 51.3 us -> 4.41 us
  other arithmetic: 20.2 us -> 0 us
  between operations: 6.74 us -> 0.65 us
    all_to_all x6 -> x0, blocking collectives: 121 us -> none  [the longest x4 82 us: from_everyone(): lax.all_to_all(jnp.broadcast_to(array[None], (devices, *array.shape)), ax...]
    pallas_call x0 -> x1, Pallas kernels: none -> 106 us  [local(): pl.pallas_call(functools.partial(kernel, dims), out_shape=(jax.ShapeDtype...]
    all_to_all x12 -> x0, waiting for transfers between devices: 90 us -> none  [the longest x8 59.1 us: from_everyone(): lax.all_to_all(jnp.broadcast_to(array[None], (devices, *array.shape)), ax...]
    all_to_all x12 -> x0, starting transfers between devices: 73.4 us -> none  [the longest x8 48.8 us: from_everyone(): lax.all_to_all(jnp.broadcast_to(array[None], (devices, *array.shape)), ax...]
    another operation x3 -> x0, loops' own time: 58.5 us -> none  [tile_pass(): return lax.fori_loop(0, slots, one, start)]
    dot_general x60 -> x0, matrix products: 50.3 us -> none  [the longest x18 28.9 us: one(): lax.dot_general(user_tile, item_tile, (((1,), (1,)), ((), ())), preferred...]
    ppermute x2 -> x0, waiting for transfers between devices: 20.5 us -> none  [shifted(): lax.ppermute(array, axis, [(i, (i + by) % devices) for i in range(devices)])]
    dynamic_slice x18 -> x0, local copies, waits for them, and re-layouts: 11.1 us -> none  [one(): code = codes[step]]
  transfers between devices with their start and end apart: 14 -> 0, of which waited for: 11 -> 0; matrix products, arithmetic and copies ran while one was open for 11% -> 0% of each run, Pallas kernels for 0% -> 0%
where the time goes in v1:
time: 112 us; the launch traced here: 111 us
  Pallas kernels  106 us (95%)
  local copies, waits for them, and re-layouts  4.41 us (4%)
    pallas_call x1, Pallas kernels, local(): pl.pallas_call(functools.partial(kernel, dims), out_shape=(jax.ShapeDtype...  106 us
    unnamed x8, local copies, waits for them, and re-layouts  4.41 us

profile of v1, /device:TPU:1, one launch (start us, length us, event | category | flops | bytes accessed | tf_op | source)
XLA Modules:
  0.0 110.9 jit_solution(10712891499958663726)
XLA Ops:
  0.6 1.3 %copy.12.index_ref = s32[1,3,6]{2,1,0:T(4,128)} copy(s32[1,3,6]{2,0,1:T(1,128)} %param.10) | data formatting | bytes 144 | tf_op args[1]
  1.9 105.9 %sweep.1 = (f32[384,256]{1,0:T(8,128)}, f32[384,256]{1,0:T(8,128)}, f32[2,256]{1,0:T(2,128)}) custom-call(s32[1,3,6]{2,1,0:T(4,128)} %copy.12.index_ref, s32[1,3]{1,0:T(1,128)} %count_ref.1, bf16[1,3,6,128,128]{4,3,2,1,0:T(8,128)(2,1)} %ratings_hbm.1, bf16[384,1024]{1,0:T(8,128)(2,1)} %feat_hbm.1, f32[384,256]{1,0:T(8,128)} %users_hbm.1, ...), custom_call_target="tpu_custom_call" | custom-call | tf_op jit(solution)/shard_map/sweep/pallas_call | solution.py:418
  107.8 0.0 copy-start
  107.8 1.8 %copy.16 = f32[384,256]{1,0:T(8,128)} copy(f32[384,256]{1,0:T(8,128)} %get-tuple-element.6) | data formatting | bytes 786432
  109.6 0.0 copy-done
  109.6 0.0 copy-start.1
  109.6 0.7 copy.17
  110.4 0.0 copy-done.1
  110.4 0.6 copy.18
Async XLA Ops:
  107.8 1.8 %copy-start = (f32[384,256]{1,0:T(8,128)S(1)}, f32[384,256]{1,0:T(8,128)}, u32[]{:S(2)}) copy-start(f32[384,256]{1,0:T(8,128)} %get-tuple-element.7) | copy-start | bytes 1179652
  109.6 0.8 copy-start.1

commit v2 on v1

v2 whole, which is shorter than its diff:
```python
import functools
import math

import jax
import jax.numpy as jnp
from jax import lax
from jax.experimental import pallas as pl
from jax.experimental.pallas import tpu as pltpu
from jax.sharding import Mesh
from jax.sharding import PartitionSpec as P

USER = ("user_0", "user_1", "user_2", "user_3")
MESH = pl.DeviceIdType.MESH
F32 = jnp.float32
BF16 = jnp.bfloat16

step_size = 0.01
prior_prec = 8.0
item_prec = 1.0
weight_decay = 1.0
rate_scale = 0.04


def nt(a, b):
    return lax.dot_general(a, b, (((1,), (1,)), ((), ())), preferred_element_type=F32)


def tn(a, b):
    return lax.dot_general(a, b, (((0,), (0,)), ((), ())), preferred_element_type=F32)


def kernel(
    dims,
    index_ref, count_ref, ratings_hbm, feat_hbm, users_hbm, items_hbm, weights_hbm, unoise_hbm, inoise_hbm,
    users_out, items_out, weights_out,
    ratings, feat, featT, feat_out, feat_in, users, users_in, items, new_items, w0, wb, unoise, inoise, mean, mean_send,
    off, err_b, grad_u, grad_v, ce_send, ce_in, g_sum, plane_in, z_out, z_in, w_own, wz, wfull,
    pay, sse_plane, pay2, sse_z, fin,
    load, ce_s, ce_r, fx_s, fx_r, ux_s, ux_r, mx_s, mx_r, prs_s, prs_r, zrs_s, zrs_r,
    zag_s, zag_r, pag_s, pag_r, sp_s, sp_r, sz_s, sz_r, sh_s, sh_r, fin_s, fin_r, met,
):
    NZ, NX, NY, strata, slots, tile, rows, featn, rank = dims
    NP = NX * NY
    half = rank // 2
    grid = rows // tile
    T2 = NZ // 2
    R8 = featn // (T2 * NP)
    jobs = 3
    pairs_z = T2 // 2
    span = featn // T2
    rate = rate_scale / (rows * NZ * NP * 2)
    noise_scale = math.sqrt(2.0 * step_size)

    z = lax.axis_index("user_0")
    x = lax.axis_index("user_1")
    y = lax.axis_index("user_2")
    c = lax.axis_index("user_3")
    p = x * NY + y
    par = lax.rem(y, 2)
    yh = y // 2
    owner = lax.rem(z + y, 2) == 0
    other = jnp.logical_not(owner)
    partner = (z, x, y, 1 - c)

    def plane_peer(i):
        return lax.rem(x + i // NY, NX), lax.rem(y + lax.rem(i, NY), NY)

    xs = [lax.rem(x + d, NX) for d in range(NX)]
    ys = [lax.rem(y + d, NY) for d in range(NY)]
    yhs = [v // 2 for v in ys]
    pars = [par, 1 - par]
    order = sorted(((dx, dy) for dx in range(NX) for dy in range(NY) if dx or dy),
                   key=lambda d: -min(d[0], NX - d[0]) - min(d[1], NY - d[1]))
    peers = [(xs[dx], ys[dy], dy % 2, yhs[dy]) for dx, dy in order]

    def device_of(idx):
        cc = lax.rem(idx, 2)
        k = idx // 2
        yy = lax.rem(k, NY)
        k = k // NY
        return (k // NX, lax.rem(k, NX), yy, cc)

    total = NZ * NP * 2
    me = (z * NP + p) * 2 + c
    nxt = device_of(lax.rem(me + 1, total))
    prv = device_of(lax.rem(me + total - 1, total))

    share = plane_in.at[0, :, pl.ds(0, NP - 1)]

    def bytes_wait(ref, sem):
        pltpu.make_async_copy(ref, ref, sem).wait()

    def remote(src, dst, s_sem, r_sem, dev):
        return pltpu.make_async_remote_copy(src_ref=src, dst_ref=dst, send_sem=s_sem, recv_sem=r_sem,
                                            device_id=dev, device_id_type=MESH)

    pairs = ((feat_hbm, feat.at[pl.ds(0, rows)]), (weights_hbm, w0),
             (users_hbm.at[:, pl.ds(0, half)], users.at[0, 0]), (users_hbm.at[:, pl.ds(half, half)], users.at[0, 1]),
             (items_hbm, items.at[0]), (ratings_hbm.at[0], ratings), (unoise_hbm, unoise), (inoise_hbm, inoise))
    loads = [pltpu.make_async_copy(a, b, load.at[i]) for i, (a, b) in enumerate(pairs)]
    for cp in loads[:4]:
        cp.start()

    barrier = pltpu.get_barrier_semaphore()

    def hello(dev):
        pl.semaphore_signal(barrier, inc=1, device_id=dev, device_id_type=MESH)

    def hello_plane(i, _):
        xx, yy = plane_peer(i)
        hello((z, xx, yy, c))
        hello((z, xx, yy, 1 - c))
        return 0

    def hello_z(i, _):
        hello((lax.rem(z + i, NZ), x, y, c))
        return 0

    reach = NZ // 4
    far_z = 2 * reach < NZ - 1
    for dz in range(reach, 0, -1):
        hello_z(dz, 0)
        hello_z(NZ - dz, 0)
    n_hello = 2 * (NP - 1) + 2 * reach + 3
    lax.fori_loop(1, NP, hello_plane, 0)
    hello(partner)
    hello(nxt)
    hello(prv)
    for cp in loads[4:]:
        cp.start()

    def tile_pass(s):
        ub = jnp.concatenate([users[s, 0].astype(BF16), users[s, 1].astype(BF16)], axis=1)
        hb = items[s].astype(BF16)
        count = count_ref[0, s]
        sse = jnp.zeros((1, tile), F32)
        for r in range(grid):
            pred = nt(ub[r * tile:(r + 1) * tile], hb)
            parts = []
            for col in range(grid):
                k = r * grid + col
                slot = jnp.int32(0)
                live = jnp.float32(0.0)
                for t in range(slots):
                    hit = index_ref[s, 0, t] == k
                    slot = jnp.where(hit, jnp.int32(t), slot)
                    live = jnp.where(jnp.logical_and(hit, t < count), jnp.float32(1.0), live)
                e = live * (ratings[s, slot].astype(F32) - pred[:, col * tile:(col + 1) * tile])
                sse = sse + jnp.sum(e * e, axis=0, keepdims=True)
                parts.append(e.astype(BF16))
            row = jnp.concatenate(parts, axis=1)
            err_b[r * tile:(r + 1) * tile, :] = row
            grad_u[r * tile:(r + 1) * tile, :] = jnp.dot(row, hb, preferred_element_type=F32)
        grad_v[...] = tn(err_b[...], ub)
        pay[s, 0:1, :] = sse
        pay[s, 1:2, :] = jnp.broadcast_to(count.astype(F32) * float(tile * tile) / float(tile), (1, tile))

    def sse_z_send(s):
        def body(i, _):
            remote(pay.at[s], sse_z.at[s, z], sz_s.at[s], sz_r.at[s], (lax.rem(z + i, NZ), x, y, c)).start()
            return 0

        lax.fori_loop(1, NZ, body, 0)
        sse_z[s, z] = pay[s]

    def sse_plane_send(s):
        bytes_wait(sse_z.at[s, pl.ds(0, NZ - 1)], sz_r.at[s])
        tot = jnp.sum(sse_z[s], axis=0)
        pay2[s] = tot
        slot = p * 2 + c
        dst = sse_plane.at[s, slot]
        sse_plane[s, slot] = tot
        for xx, yy, d, yyh in peers:
            for cc in (c, 1 - c):
                remote(pay2.at[s], dst, sp_s.at[s], sp_r.at[s], (z, xx, yy, cc)).start()
        remote(pay2.at[s], dst, sp_s.at[s], sp_r.at[s], partner).start()

    def precision_of(s):
        bytes_wait(sse_plane.at[s, pl.ds(0, 2 * NP - 1)], sp_r.at[s])
        tot = jnp.sum(sse_plane[s], axis=0)
        sums = jnp.sum(tot, axis=1, keepdims=True)
        return (1.0 + sums[1:2, :] / 2.0) / (1.0 + sums[0:1, :] / 2.0)

    def update_items(s, precision):
        h = items[s]
        dst = new_items.at[s] if s + 1 < strata else items_out
        dst[...] = (h + step_size * (jnp.broadcast_to(precision, (1, rank)) * grad_v[...] - item_prec * h)
                        + noise_scale * inoise[s].astype(F32))

    def shift(s):
        remote(new_items.at[s], items.at[s + 1], sh_s.at[s], sh_r.at[s], nxt).start()

    def update_users(s, precision):
        pr = jnp.broadcast_to(precision, (1, half))
        for h in range(2):
            u = users[s, h]
            cols = slice(h * half, (h + 1) * half)
            new = (u + step_size * (pr * grad_u[:, cols] - prior_prec * (u - mean[s, h]))
                   + noise_scale * unoise[s][:, cols].astype(F32))
            if s + 1 < strata:
                users[s + 1, h] = new
            else:
                users_out[:, cols] = new

    def users_to_partner(s):
        remote(users.at[s, 1 - c], users_in.at[s - 1], ux_s.at[s - 1], ux_r.at[s - 1], partner).start()

    odd = lax.rem(z, 2)

    def pair(j):
        up = T2 // 2 + j * (1 - 2 * odd)
        down = T2 // 2 - 1 - j + odd * (2 + 2 * j)
        return lax.rem(z // 2 + up, T2), lax.rem(z // 2 + down, T2)

    groups = [t for j in range(pairs_z) for t in pair(j)]

    def group(ref, t):
        return ref[pl.ds(pl.multiple_of(t * span, 128), span), :]

    def group_send(k, i, t):
        for xx, yy, d, yyh in peers:
            remote(g_sum.at[k, t, pars[d], xx, yyh], plane_in.at[k, i, p], prs_s.at[k], prs_r.at[k, i], (z, xx, yy, c)).start()
        plane_in[k, i, p] = g_sum[k, t, par, x, yh]

    def plane_sum_z_send(k):
        for i, t in enumerate(groups):
            bytes_wait(plane_in.at[k, i, pl.ds(0, NP - 1)], prs_r.at[k, i])
            acc = plane_in[k, i, 0]
            for q in range(1, NP):
                acc = acc + plane_in[k, i, q]
            z_out[k, i] = acc

            def send():
                remote(z_out.at[k, i], z_in.at[k, z], zrs_s.at[k], zrs_r.at[k], (2 * t + par, x, y, c)).start()

            if i == T2 - 1:
                pl.when(other)(send)
            else:
                send()

    def z_sum(k):
        z_in[k, z] = z_out[k, T2 - 1]
        bytes_wait(z_in.at[k, pl.ds(0, NZ - 1)], zrs_r.at[k])
        g = z_in[k, 0]
        for n in range(1, NZ):
            g = g + z_in[k, n]
        return g

    def step_weights(g):
        w = w_own[...]
        w = w + rate * (prior_prec * g - weight_decay * w)
        w_own[...] = w
        return w

    def weights_along_z(s):
        @pl.when(owner)
        def _():
            wz[s, z // 2] = step_weights(z_sum(s))

            def body(i, _):
                for d in (T2 - i, T2 + i):
                    remote(wz.at[s, z // 2], wz.at[s, z // 2], zag_s.at[s], zag_r.at[s, z // 2],
                           (lax.rem(z + d, NZ), x, y, c)).start()
                return 0

            remote(wz.at[s, z // 2], wz.at[s, z // 2], zag_s.at[s], zag_r.at[s, z // 2],
                   (lax.rem(z + T2, NZ), x, y, c)).start()
            lax.fori_loop(1, T2, body, 0)

    def weights_over_plane(s):
        for j in range(pairs_z - 1, -1, -1):
            for n, t in reversed(tuple(enumerate(pair(j)))):
                def arrived():
                    bytes_wait(wz.at[s, t], zag_r.at[s, t])

                if j == pairs_z - 1 and n == 1:
                    pl.when(other)(arrived)
                else:
                    arrived()
                for xx, yy, d, yyh in peers:
                    remote(wz.at[s, t], wfull.at[s, t, par, x, yh], pag_s.at[s], pag_r.at[s, j], (z, xx, yy, c)).start()
                wfull[s, t, par, x, yh] = wz[s, t]

    def mean_of_both(s):
        acc = None
        for j in range(pairs_z - 1, -1, -1):
            bytes_wait(share.at[pl.ds(0, 2)], pag_r.at[s, j])
            t0, t1 = pair(j)
            w = jnp.concatenate([wfull[s, t].reshape(span, half).astype(BF16) for t in (t0, t1)], axis=0)
            f = jnp.concatenate([feat[:, pl.ds(pl.multiple_of(t * span, 128), span)] for t in (t0, t1)], axis=1)
            part = jnp.dot(f, w, preferred_element_type=F32)
            acc = part if acc is None else acc + part
        return acc

    def means_to_partner(s, m):
        mean_send[s - 1] = m[rows:]
        remote(mean_send.at[s - 1], mean.at[s, c], mx_s.at[s - 1], mx_r.at[s - 1], partner).start()

    loads[0].wait()
    loads[1].wait()
    wb[...] = w0[...].astype(BF16)
    for i in range(rows // 128):
        featT[:, i * 128:(i + 1) * 128] = feat[i * 128:(i + 1) * 128, :].T
    t_own = z * (NP // 2) + p // 2
    own8 = w0[pl.ds(pl.multiple_of(t_own * R8, 8), R8), :]
    w_own[...] = jnp.where(c == 0, own8[:, :half], own8[:, half:])
    m = jnp.dot(feat[0:rows], wb[...], preferred_element_type=F32)
    loads[2].wait()
    loads[3].wait()
    for h in range(2):
        mh = m[:, h * half:(h + 1) * half]
        mean[0, h] = mh
        off[h] = (users[0, h] - mh).astype(BF16)
    shape = ce_send.shape[1:]
    for i, t in enumerate(groups):
        ce_send[t] = jnp.dot(group(featT, t)[:, 0:rows], off[1 - c], preferred_element_type=F32).reshape(shape)
        if i == 0:
            pl.semaphore_wait(barrier, n_hello)
            if far_z:
                for dz in (reach, NZ - reach):
                    pl.semaphore_signal(met, inc=1, device_id=(lax.rem(z + dz, NZ), x, y, c), device_id_type=MESH)
        remote(ce_send.at[t], ce_in.at[t], ce_s, ce_r.at[i], partner).start()
    for i, t in enumerate(groups):
        g = jnp.dot(group(featT, t)[:, 0:rows], off[c], preferred_element_type=F32).reshape(shape)
        bytes_wait(ce_in.at[t], ce_r.at[i])
        g_sum[0, t] = g + ce_in[t]
        group_send(0, i, t)
    loads[4].wait()
    loads[5].wait()
    tile_pass(0)
    if far_z:
        pl.semaphore_wait(met, 2)
    sse_z_send(0)
    feat_out[...] = feat[0:rows].astype(F32)
    remote(feat_out, feat_in, fx_s, fx_r, partner).start()
    plane_sum_z_send(0)
    sse_plane_send(0)
    bytes_wait(feat_in, fx_r)
    feat[rows:, :] = feat_in[...].astype(BF16)
    for i in range(rows // 128):
        featT[:, rows + i * 128:rows + (i + 1) * 128] = feat[rows + i * 128:rows + (i + 1) * 128, :].T
    for cp in loads[6:]:
        cp.wait()
    for s in range(strata - 1):
        weights_along_z(s)
        weights_over_plane(s)
        precision = precision_of(s)
        update_items(s, precision)
        shift(s)
        if s > 0:
            bytes_wait(mean.at[s, 0], mx_r.at[s - 1])
        update_users(s, precision)
        users_to_partner(s + 1)
        n = s + 1
        m = mean_of_both(s)
        bytes_wait(users_in.at[s], ux_r.at[s])
        o = jnp.concatenate([users[n, c] - m[:rows], users_in[s] - m[rows:]], axis=0).astype(BF16)

        def send_groups(some):
            for i in some:
                t = groups[i]
                g_sum[n, t] = jnp.dot(group(featT, t), o, preferred_element_type=F32).reshape(shape)
                group_send(n, i, t)

        send_groups(range(T2 // 2))
        bytes_wait(items.at[n], sh_r.at[s])
        tile_pass(n)
        sse_z_send(n)
        send_groups(range(T2 // 2, T2))
        mean[n, c] = m[:rows]
        means_to_partner(n, m)
        plane_sum_z_send(n)
        sse_plane_send(n)

    @pl.when(owner)
    def _():
        w = step_weights(z_sum(strata - 1))
        fin[c] = w
        for n, dev in enumerate((partner, (z, x, y + 1 - 2 * par, c), (z, x, y + 1 - 2 * par, 1 - c))):
            remote(w_own, fin.at[c], fin_s.at[n], fin_r.at[c], dev).start()

    e = strata - 1
    bytes_wait(mean.at[e, 0], mx_r.at[e - 1])
    precision = precision_of(e)
    update_items(e, precision)
    update_users(e, precision)

    @pl.when(owner)
    def _():
        bytes_wait(fin.at[0], fin_r.at[1 - c])

    @pl.when(other)
    def _():
        bytes_wait(fin.at[0], fin_r.at[0])
        bytes_wait(fin.at[1], fin_r.at[1])

    r2 = R8 // 4
    for h in range(2):
        t8 = fin[h]
        o2 = t8[0:r2]
        for k in range(1, 4):
            o2 = jnp.where(par * 2 + c == k, t8[r2 * k:r2 * (k + 1)], o2)
        weights_out[:, h * half:(h + 1) * half] = o2

    bytes_wait(ce_send, ce_s)
    bytes_wait(feat_out, fx_s)
    for s in range(strata - 1):
        bytes_wait(users_in.at[s], ux_s.at[s])
        bytes_wait(mean_send.at[s], mx_s.at[s])
        bytes_wait(new_items.at[s], sh_s.at[s])
        bytes_wait(share, pag_s.at[s])
    for k in range(jobs):
        bytes_wait(share, prs_s.at[k])

    @pl.when(owner)
    def _():
        for k in range(jobs):
            bytes_wait(z_out.at[k, pl.ds(0, T2 - 1)], zrs_s.at[k])
        for s in range(strata - 1):
            bytes_wait(z_in.at[s, pl.ds(0, NZ - 1)], zag_s.at[s])
        for n in range(3):
            bytes_wait(w_own, fin_s.at[n])

    @pl.when(other)
    def _():
        for k in range(jobs):
            bytes_wait(z_out.at[k], zrs_s.at[k])

    for s in range(strata):
        bytes_wait(sse_plane.at[s, pl.ds(0, 2 * NP - 1)], sp_s.at[s])
        bytes_wait(sse_z.at[s, pl.ds(0, NZ - 1)], sz_s.at[s])


def local(ratings, tile_index, tile_count, side, users, items, weights, unoise, inoise):
    nz, nx, ny = (lax.axis_size(a) for a in USER[:3])
    strata, slots, tile = ratings.shape[1:4]
    rows, rank = users.shape
    featn = side.shape[1]
    npl, t2, half = nx * ny, nz // 2, rank // 2
    r8 = featn // (t2 * npl)
    jobs = 3
    dims = (nz, nx, ny, strata, slots, tile, rows, featn, rank)
    g_shape = (t2, 2, nx, ny // 2, r8, half)
    V, D = pltpu.VMEM, pltpu.SemaphoreType.DMA
    data = [
        V((strata, slots, tile, tile), BF16),
        V((2 * rows, featn), BF16),
        V((featn, 2 * rows), BF16),
        V((rows, featn), F32),
        V((rows, featn), F32),
        V((strata, 2, rows, half), F32),
        V((strata - 1, rows, half), F32),
        V((strata, rows, rank), F32),
        V((strata - 1, rows, rank), F32),
        V((featn, rank), F32),
        V((featn, rank), BF16),
        V((strata, rows, rank), BF16),
        V((strata, rows, rank), BF16),
        V((strata, 2, rows, half), F32),
        V((strata - 1, rows, half), F32),
        V((2, rows, half), BF16),
        V((rows, rows), BF16),
        V((rows, rank), F32),
        V((rows, rank), F32),
        V(g_shape, F32),
        V(g_shape, F32),
        V((jobs, *g_shape), F32),
        V((jobs, t2, npl, r8, half), F32),
        V((jobs, t2, r8, half), F32),
        V((jobs, nz, r8, half), F32),
        V((r8, half), F32),
        V((strata - 1, t2, r8, half), F32),
        V((strata - 1, *g_shape), F32),
        V((strata, 2, tile), F32),
        V((strata, 2 * npl, 2, tile), F32),
        V((strata, 2, tile), F32),
        V((strata, nz, 2, tile), F32),
        V((2, r8, half), F32),
    ]
    sems = [
        D((8,)),
        D(()), D((t2,)),
        D(()), D(()),
        D((strata - 1,)), D((strata - 1,)),
        D((strata - 1,)), D((strata - 1,)),
        D((jobs,)), D((jobs, t2)),
        D((jobs,)), D((jobs,)),
        D((strata - 1,)), D((strata - 1, t2)),
        D((strata - 1,)), D((strata - 1, t2 // 2)),
        D((strata,)), D((strata,)),
        D((strata,)), D((strata,)),
        D((strata - 1,)), D((strata - 1,)),
        D((3,)), D((2,)),
        pltpu.SemaphoreType.REGULAR,
    ]
    any_ = pl.BlockSpec(memory_space=pltpu.HBM)
    vmem = pl.BlockSpec(memory_space=pltpu.VMEM)
    smem = pl.BlockSpec(memory_space=pltpu.SMEM)
    return pl.pallas_call(
        functools.partial(kernel, dims),
        out_shape=(
            jax.ShapeDtypeStruct((rows, rank), F32),
            jax.ShapeDtypeStruct((rows, rank), F32),
            jax.ShapeDtypeStruct((r8 // 4, rank), F32),
        ),
        in_specs=[smem, smem] + [any_] * 7,
        out_specs=(vmem, vmem, vmem),
        scratch_shapes=data + sems,
        compiler_params=pltpu.CompilerParams(collective_id=0, has_side_effects=True, vmem_limit_bytes=53 * 1024 * 1024),
        name="sweep",
    )(jnp.transpose(tile_index, (1, 0, 2)), tile_count, ratings, side, users, items, weights, unoise, inoise)


def finer_of(mesh):
    return Mesh(mesh.devices.reshape(16, 4, 4, 2), USER)


def solution(mesh):
    return over(finer_of(mesh))


def over(finer):
    return jax.shard_map(
        local,
        mesh=finer,
        in_specs=(
            P(USER, None, None, None, None),
            P(USER, None, None),
            P(USER, None),
            P(USER, None),
            P(USER, None),
            P(USER, None),
            P(),
            P(None, USER, None),
            P(None, USER, None),
        ),
        out_specs=(P(USER, None), P(USER, None), P(USER, None)),
        check_vma=False,
    )
```

time: 112 us -> 95.7 us (0.85)
  Pallas kernels: 106 us -> 91.5 us
    pallas_call x1, Pallas kernels: 106 us -> 91.5 us  [local(): pl.pallas_call(functools.partial(kernel, dims), out_shape=(jax.ShapeDtype...]
    unnamed x8 -> x7, local copies, waits for them, and re-layouts: 4.41 us -> 3.4 us
where the time goes in v2:
time: 95.7 us; the launch traced here: 95.6 us
  Pallas kernels  91.5 us (96%)
  local copies, waits for them, and re-layouts  3.4 us (4%)
    pallas_call x1, Pallas kernels, local(): pl.pallas_call(functools.partial(kernel, dims), out_shape=(jax.ShapeDtype...  91.5 us
    unnamed x7, local copies, waits for them, and re-layouts  3.4 us

profile of v2, /device:TPU:1, one launch (start us, length us, event | category | flops | bytes accessed | tf_op | source)
XLA Modules:
  0.0 95.6 jit_solution(3025724170710674071)
XLA Ops:
  0.6 0.0 copy-start
  0.6 0.7 copy-done
  1.3 0.0 copy-start.1
  1.3 0.7 copy-done.1
  2.0 91.5 %sweep.1 = (f32[384,256]{1,0:T(8,128)S(1)}, f32[384,256]{1,0:T(8,128)S(1)}, f32[2,256]{1,0:T(2,128)S(1)}) custom-call(s32[3,1,6]{2,1,0:T(1,128)S(1)} %bitcast.1, s32[1,3]{1,0:T(1,128)S(1)} %copy-done.1, bf16[1,3,6,128,128]{4,3,2,1,0:T(8,128)(2,1)} %ratings_hbm.1, bf16[384,1024]{1,0:T(8,128)(2,1)} %feat_hbm.1, f32[384,256]{1,0:T(8,128)} %users_hbm.1, ...), custom_call_target="tpu_custom_call" | custom-call | tf_op jit(solution)/shard_map/sweep/pallas_call | solution.py:499
  93.5 0.7 copy.15
  94.2 0.7 copy.16
  95.0 0.6 copy.17
Async XLA Ops:
  0.6 0.7 copy-start
  1.3 0.7 copy-start.1

commit v3 on v2

--- a/solution.py
+++ b/solution.py
@@ -222,8 +222,9 @@
             remote(g_sum.at[k, t, pars[d], xx, yyh], plane_in.at[k, i, p], prs_s.at[k], prs_r.at[k, i], (z, xx, yy, c)).start()
         plane_in[k, i, p] = g_sum[k, t, par, x, yh]
 
-    def plane_sum_z_send(k):
-        for i, t in enumerate(groups):
+    def plane_sum_z_send(k, some):
+        for i in some:
+            t = groups[i]
             bytes_wait(plane_in.at[k, i, pl.ds(0, NP - 1)], prs_r.at[k, i])
             acc = plane_in[k, i, 0]
             for q in range(1, NP):
@@ -267,19 +268,20 @@
                    (lax.rem(z + T2, NZ), x, y, c)).start()
             lax.fori_loop(1, T2, body, 0)
 
-    def weights_over_plane(s):
-        for j in range(pairs_z - 1, -1, -1):
-            for n, t in reversed(tuple(enumerate(pair(j)))):
-                def arrived():
-                    bytes_wait(wz.at[s, t], zag_r.at[s, t])
-
-                if j == pairs_z - 1 and n == 1:
-                    pl.when(other)(arrived)
-                else:
-                    arrived()
-                for xx, yy, d, yyh in peers:
-                    remote(wz.at[s, t], wfull.at[s, t, par, x, yh], pag_s.at[s], pag_r.at[s, j], (z, xx, yy, c)).start()
-                wfull[s, t, par, x, yh] = wz[s, t]
+    def weights_over_plane(s, some):
+        for i in some:
+            t = groups[i]
+
+            def arrived():
+                bytes_wait(wz.at[s, t], zag_r.at[s, t])
+
+            if i == T2 - 1:
+                pl.when(other)(arrived)
+            else:
+                arrived()
+            for xx, yy, d, yyh in peers:
+                remote(wz.at[s, t], wfull.at[s, t, par, x, yh], pag_s.at[s], pag_r.at[s, i // 2], (z, xx, yy, c)).start()
+            wfull[s, t, par, x, yh] = wz[s, t]
 
     def mean_of_both(s):
         acc = None
@@ -312,19 +314,23 @@
         mean[0, h] = mh
         off[h] = (users[0, h] - mh).astype(BF16)
     shape = ce_send.shape[1:]
-    for i, t in enumerate(groups):
-        ce_send[t] = jnp.dot(group(featT, t)[:, 0:rows], off[1 - c], preferred_element_type=F32).reshape(shape)
-        if i == 0:
-            pl.semaphore_wait(barrier, n_hello)
-            if far_z:
-                for dz in (reach, NZ - reach):
-                    pl.semaphore_signal(met, inc=1, device_id=(lax.rem(z + dz, NZ), x, y, c), device_id_type=MESH)
-        remote(ce_send.at[t], ce_in.at[t], ce_s, ce_r.at[i], partner).start()
-    for i, t in enumerate(groups):
-        g = jnp.dot(group(featT, t)[:, 0:rows], off[c], preferred_element_type=F32).reshape(shape)
-        bytes_wait(ce_in.at[t], ce_r.at[i])
-        g_sum[0, t] = g + ce_in[t]
-        group_send(0, i, t)
+    lag = 3
+    for n in range(T2 + lag):
+        if n < T2:
+            t = groups[n]
+            ce_send[t] = jnp.dot(group(featT, t)[:, 0:rows], off[1 - c], preferred_element_type=F32).reshape(shape)
+            if n == 0:
+                pl.semaphore_wait(barrier, n_hello)
+                if far_z:
+                    for dz in (reach, NZ - reach):
+                        pl.semaphore_signal(met, inc=1, device_id=(lax.rem(z + dz, NZ), x, y, c), device_id_type=MESH)
+            remote(ce_send.at[t], ce_in.at[t], ce_s, ce_r.at[n], partner).start()
+        if n >= lag:
+            i, t = n - lag, groups[n - lag]
+            g = jnp.dot(group(featT, t)[:, 0:rows], off[c], preferred_element_type=F32).reshape(shape)
+            bytes_wait(ce_in.at[t], ce_r.at[i])
+            g_sum[0, t] = g + ce_in[t]
+            group_send(0, i, t)
     loads[4].wait()
     loads[5].wait()
     tile_pass(0)
@@ -333,7 +339,7 @@
     sse_z_send(0)
     feat_out[...] = feat[0:rows].astype(F32)
     remote(feat_out, feat_in, fx_s, fx_r, partner).start()
-    plane_sum_z_send(0)
+    plane_sum_z_send(0, range(T2))
     sse_plane_send(0)
     bytes_wait(feat_in, fx_r)
     feat[rows:, :] = feat_in[...].astype(BF16)
@@ -343,14 +349,15 @@
         cp.wait()
     for s in range(strata - 1):
         weights_along_z(s)
-        weights_over_plane(s)
+        weights_over_plane(s, range(T2 - 1, T2 // 2 - 2, -1))
         precision = precision_of(s)
-        update_items(s, precision)
-        shift(s)
         if s > 0:
             bytes_wait(mean.at[s, 0], mx_r.at[s - 1])
         update_users(s, precision)
         users_to_partner(s + 1)
+        update_items(s, precision)
+        weights_over_plane(s, range(T2 // 2 - 2, -1, -1))
+        shift(s)
         n = s + 1
         m = mean_of_both(s)
         bytes_wait(users_in.at[s], ux_r.at[s])
@@ -362,15 +369,18 @@
                 g_sum[n, t] = jnp.dot(group(featT, t), o, preferred_element_type=F32).reshape(shape)
                 group_send(n, i, t)
 
-        send_groups(range(T2 // 2))
+        first = T2 // 2 if n + 1 < strata else T2 // 4
+        send_groups(range(first))
         bytes_wait(items.at[n], sh_r.at[s])
         tile_pass(n)
         sse_z_send(n)
-        send_groups(range(T2 // 2, T2))
+        send_groups(range(first, T2))
         mean[n, c] = m[:rows]
         means_to_partner(n, m)
-        plane_sum_z_send(n)
+        cut = T2 if n + 1 < strata else T2 // 2 + 1
+        plane_sum_z_send(n, range(cut))
         sse_plane_send(n)
+        plane_sum_z_send(n, range(cut, T2))
 
     @pl.when(owner)
     def _():
@@ -429,6 +439,10 @@
     for s in range(strata):
         bytes_wait(sse_plane.at[s, pl.ds(0, 2 * NP - 1)], sp_s.at[s])
         bytes_wait(sse_z.at[s, pl.ds(0, NZ - 1)], sz_s.at[s])
+
+
+def in_place(array):
+    return pltpu.with_memory_space_constraint(array, pltpu.HBM)
 
 
 def local(ratings, tile_index, tile_count, side, users, items, weights, unoise, inoise):
@@ -508,7 +522,7 @@
         scratch_shapes=data + sems,
         compiler_params=pltpu.CompilerParams(collective_id=0, has_side_effects=True, vmem_limit_bytes=53 * 1024 * 1024),
         name="sweep",
-    )(jnp.transpose(tile_index, (1, 0, 2)), tile_count, ratings, side, users, items, weights, unoise, inoise)
+    )(in_place(jnp.transpose(tile_index, (1, 0, 2))), in_place(tile_count), ratings, side, users, items, weights, unoise, inoise)
 
 
 def finer_of(mesh):

time: 95.7 us -> 93.6 us (0.978)
  local copies, waits for them, and re-layouts: 3.4 us -> 2.07 us
  Pallas kernels: 91.5 us -> 90.5 us
    unnamed x7 -> x3, local copies, waits for them, and re-layouts: 3.4 us -> 2.07 us
    pallas_call x1, Pallas kernels: 91.5 us -> 90.5 us  [local(): pl.pallas_call(functools.partial(kernel, dims), out_shape=(jax.ShapeDtype...]
where the time goes in v3:
time: 93.6 us; the launch traced here: 93.2 us
  Pallas kernels  90.5 us (97%)
  local copies, waits for them, and re-layouts  2.07 us (2%)
    pallas_call x1, Pallas kernels, local(): pl.pallas_call(functools.partial(kernel, dims), out_shape=(jax.ShapeDtype...  90.5 us
    unnamed x3, local copies, waits for them, and re-layouts  2.07 us

profile of v3, /device:TPU:1, one launch (start us, length us, event | category | flops | bytes accessed | tf_op | source)
XLA Modules:
  0.0 93.2 jit_solution(16354463822280918069)
XLA Ops:
  0.6 90.5 %sweep.1 = (f32[384,256]{1,0:T(8,128)S(1)}, f32[384,256]{1,0:T(8,128)S(1)}, f32[2,256]{1,0:T(2,128)S(1)}) custom-call(s32[3,1,6]{2,1,0:T(1,128)} %bitcast.1, s32[1,3]{1,0:T(1,128)} %count_ref.1, bf16[1,3,6,128,128]{4,3,2,1,0:T(8,128)(2,1)} %ratings_hbm.1, bf16[384,1024]{1,0:T(8,128)(2,1)} %feat_hbm.1, f32[384,256]{1,0:T(8,128)} %users_hbm.1, ...), custom_call_target="tpu_custom_call" | custom-call | tf_op jit(solution)/shard_map/sweep/pallas_call | solution.py:513
  91.2 0.7 copy.15
  91.9 0.7 copy.16
  92.7 0.6 copy.17
